TPU v7x, 32 devices: a whole 2x2x4 slice. The times are simulated.
32 devices in a mesh: amp: 4 (over y, core), own: 8 (over z, x).
Axes of the slice: x: 2, y: 2, z: 4, core: 2. Of those that a mesh axis runs over, the one named last changes fastest.
Arguments:
- amplitudes: bfloat16 [32, 2304, 192], P('own', None, 'amp'), may hold values from -6 to 6
- integrals: bfloat16 [32, 1152, 2304], P('own'), as said below
- occ_irrep: int32 [34], replicated, may hold values from 0 to 7, as said below
- tile_irrep: int32 [18], replicated, may hold values from 0 to 7, as said below
Outputs:
- cycle_term: bfloat16 [2304, 2304], P(('amp', 'own'))
Inputs may be any that keep to these rules, and one draw needn't show every extreme that they name: `occ_irrep`: labels of the D2h group, combined by XOR; every label occurs, and all labels occur equally often up to one. `tile_irrep`: labels of the D2h group, combined by XOR; every label occurs, and all labels occur equally often up to one, so some label has exactly 3 tiles. integrals[k, c, (j, b)] is zero unless the labels of k, c, j and b combine by XOR to 0.
All inputs are finite; a program needn't handle non-finite values.
Results may differ from a plain program's by a relative error of at most 0.001.
Values may be sent and summed in bfloat16 or wider, within the bound.
A program may use at most 128 MiB of HBM per device.

v0:
```python
import jax
import jax.numpy as jnp
from jax import lax
from jax.sharding import PartitionSpec as P

V = 1152
TILE = 64
NI = 2


def tile_ranks(tile_irrep):
    count = tile_irrep.shape[0]
    index = jnp.arange(count, dtype=jnp.int32)
    same = (tile_irrep[:, None] == tile_irrep[None, :]) & (index[None, :] < index[:, None])
    return jnp.sum(same.astype(jnp.int32), axis=1)


def shards(amplitudes, integrals, occ_irrep, tile_irrep):
    amp_index = lax.axis_index("amp")
    own_index = lax.axis_index("own")
    n_amp = lax.axis_size("amp")
    n_own = lax.axis_size("own")
    regrouped = lax.all_to_all(amplitudes, "amp", split_axis=1, concat_axis=2, tiled=True)
    k_local, rows, packed_width = regrouped.shape
    slot_count = packed_width // TILE
    virt_lab = jnp.repeat(tile_irrep, TILE)
    row_all = jnp.bitwise_xor(jnp.repeat(occ_irrep[:NI], V), jnp.tile(virt_lab, NI))
    row_lab = lax.dynamic_slice_in_dim(row_all, amp_index * rows, rows)
    k_lab = lax.dynamic_slice_in_dim(occ_irrep, NI + own_index * k_local, k_local)
    wanted = jnp.bitwise_xor(k_lab[:, None], row_lab[None, :])
    ranks = tile_ranks(tile_irrep)
    slot_ids = jnp.arange(slot_count, dtype=jnp.int32)
    select = (tile_irrep[None, None, None, :] == wanted[:, :, None, None]) & (
        ranks[None, None, None, :] == slot_ids[None, None, :, None]
    )
    pieces = regrouped.reshape(k_local, rows, slot_count, TILE)
    dense = jnp.einsum(
        "krjt,krje->krte", select.astype(jnp.bfloat16), pieces, preferred_element_type=jnp.float32
    )
    masked = dense.reshape(k_local, rows, V).astype(jnp.bfloat16)
    summed = lax.psum_scatter(
        jnp.einsum("kmc,kcn->mn", masked, integrals, preferred_element_type=jnp.float32),
        "own",
        scatter_dimension=0,
        tiled=True,
    )
    share = summed.shape[0]
    blocks = summed.reshape(share, n_amp, n_own, share)
    moved = lax.all_to_all(
        lax.all_to_all(blocks, "amp", split_axis=1, concat_axis=1, tiled=True),
        "own",
        split_axis=2,
        concat_axis=2,
        tiled=True,
    )
    mirrored = jnp.transpose(moved, (3, 1, 2, 0)).reshape(share, NI * V)
    return (summed + mirrored).astype(jnp.bfloat16)


def solution(mesh):
    return jax.shard_map(
        shards,
        mesh=mesh,
        in_specs=(P("own", None, "amp"), P("own", None, None), P(), P()),
        out_specs=P(("amp", "own"), None),
        check_vma=False,
    )
```

profile of v0, /device:TPU:0, one launch (start us, length us, event | category | flops | bytes accessed | tf_op | source)
XLA Modules:
  0.0 252.3 jit_solution(9332235532349839505)
XLA Ops:
  6.5 3.6 %copy.25 = bf16[4,2304,48]{2,0,1:T(4,128)(2,1)S(1)} copy(bf16[4,2304,48]{1,2,0:T(8,128)(2,1)} %param.4) | data formatting | bytes 1769472 | tf_op args[0]
  10.1 0.0 copy-start.1
  10.1 0.0 copy-start.2
  10.1 4.6 %reshape.80 = bf16[4,2,55296]{2,1,0:T(2,128)(2,1)} reshape(bf16[2304,4,48]{2,1,0:T(4,128)(2,1)S(1)} %bitcast.18) | data formatting | bytes 1769472
  14.8 4.2 %all-to-all-start = ((bf16[4,2,55296]{2,1,0:T(2,128)(2,1)}), bf16[4,2,55296]{2,1,0:T(2,128)(2,1)S(1)}, u32[]{:S(2)}, u32[]{:S(2)}) async-start(bf16[4,2,55296]{2,1,0:T(2,128)(2,1)} %reshape.80), calls=%async_computation | async-start | bytes 1769472 | tf_op jit(solution)/shard_map/all_to_all | solution.py:23
  19.0 0.0 reduce-scatter.2.cloned.1.call-start
  19.0 0.0 copy-done.1
  19.0 0.2 convert_reduce_fusion
  19.2 0.1 broadcast_in_dim.5
  19.3 0.1 tile.8
  19.3 0.1 dynamic_slice.6
  19.4 0.1 broadcast_xor_fusion.1
  19.5 0.1 dynamic_slice.7
  19.6 0.1 broadcast_xor_fusion
  19.7 1.1 broadcast_compare_fusion
  20.8 10.9 %all-to-all-done = bf16[4,2,55296]{2,1,0:T(2,128)(2,1)S(1)} async-done(((bf16[4,2,55296]{2,1,0:T(2,128)(2,1)}), bf16[4,2,55296]{2,1,0:T(2,128)(2,1)S(1)}, u32[]{:S(2)}, u32[]{:S(2)}) %all-to-all-start) | async-done | bytes 884768 | tf_op jit(solution)/shard_map/all_to_all | solution.py:23
  31.7 2.4 reshape.81
  34.1 1.5 copy.27
  35.6 1.5 copy.28
  37.1 11.1 %convolution_convert_fusion = bf16[4,576,18,64]{3,2,1,0:T(8,128)(2,1)} fusion(bf16[4,576,3,64]{3,2,1,0:T(4,128)(2,1)S(1)} %copy.28, pred[3,18]{1,0:T(4,128)(4,1)S(1)} %iota_compare_fusion.1, pred[4,576,18]{2,1,0:T(8,128)(4,1)} %broadcast_compare_fusion), kind=kOutput, calls=%fused_computation | convolution fusion | flops 18703872 | bytes 6234678 | tf_op jit(solution)/shard_map/krjt,krje->krte/dot_general | solution.py:37
  48.2 15.5 %copy.29 = bf16[4,576,18,64]{1,3,2,0:T(8,128)(2,1)} copy(bf16[4,576,18,64]{3,2,1,0:T(8,128)(2,1)} %convolution_convert_fusion) | data formatting | bytes 10616832 | tf_op jit(solution)/shard_map/convert_element_type | solution.py:40
  63.7 19.2 %convolution_bitcast_fusion = f32[576,2304]{1,0:T(8,128)} fusion(bf16[4,576,1152]{1,2,0:T(8,128)(2,1)} %bitcast.19, bf16[4,1152,2304]{2,1,0:T(8,128)(2,1)} %param.5), kind=kOutput, calls=%fused_computation.1 | convolution fusion | flops 12230590464 | bytes 31850496 | tf_op jit(solution)/shard_map/kmc,kcn->mn/dot_general | solution.py:42
  82.8 0.0 reduce-scatter.2.cloned.1.call-update
  82.9 105.3 %reduce-scatter.2.cloned.1.call-done = f32[72,2304]{1,0:T(8,128)} async-done(((f32[576,2304]{1,0:T(8,128)}), f32[72,2304]{1,0:T(8,128)}) %reduce-scatter.2.cloned.1.call-update) | async-done | bytes 663568 | tf_op jit(solution)/shard_map/reduce_scatter | solution.py:41
  188.2 2.3 reshape.77
  190.5 0.9 copy.31
  191.4 18.4 %all_to_all.25 = f32[72,4,8,72]{0,2,3,1:T(8,128)S(1)} all-to-all(f32[72,4,8,72]{0,2,3,1:T(8,128)S(1)} %copy.31), channel_id=1, replica_groups=mesh['amp'=4,'own'=8] {'amp'}, dimensions={1} | all-to-all | bytes 1327104 | tf_op jit(solution)/shard_map/all_to_all | solution.py:50
  209.8 0.8 copy.32
  210.6 32.7 %all_to_all.26 = f32[72,4,8,72]{0,1,3,2:T(4,128)S(1)} all-to-all(f32[72,4,8,72]{0,1,3,2:T(4,128)S(1)} %copy.32), channel_id=1, replica_groups=mesh['amp'=4,'own'=8] {'own'}, dimensions={2} | all-to-all | bytes 1327104 | tf_op jit(solution)/shard_map/all_to_all | solution.py:49
  243.3 0.7 copy.33
  244.0 0.6 reshape.78
  244.7 0.8 add_convert_fusion
  (5 shorter events, 0.0 us)
Async XLA Ops:
  10.1 8.9 %copy-start.1 = (s32[18]{0:T(128)S(1)}, s32[18]{0:T(128)}, u32[]{:S(2)}) copy-start(s32[18]{0:T(128)} %param.7) | copy-start | bytes 220
  10.1 9.2 %copy-start.2 = (s32[34]{0:T(128)S(1)}, s32[34]{0:T(128)}, u32[]{:S(2)}) copy-start(s32[34]{0:T(128)} %param.6) | copy-start | bytes 412
  14.8 16.9 %all-to-all-start = ((bf16[4,2,55296]{2,1,0:T(2,128)(2,1)}), bf16[4,2,55296]{2,1,0:T(2,128)(2,1)S(1)}, u32[]{:S(2)}, u32[]{:S(2)}) async-start(bf16[4,2,55296]{2,1,0:T(2,128)(2,1)} %reshape.80), calls=%async_computation | async-start | bytes 1769472 | tf_op jit(solution)/shard_map/all_to_all | solution.py:23
  19.0 169.2 %reduce-scatter.2.cloned.1.call-start = ((), (), s32[]{:S(2)}) async-start(), calls=%async_computation.4 | async-start | bytes 5971968 | tf_op jit(solution)/shard_map/reduce_scatter | solution.py:41
  243.3 1.3 copy-start
Sparse Core Ops, SparseCore 0:
  83.0 105.1 reduce-scatter.1
where the time goes:
time: 253 us; the launch traced here: 252 us
  waiting for transfers between devices  116 us (46%)
  blocking collectives  51.1 us (20%)
  local copies, waits for them, and re-layouts  34.7 us (14%)
  matrix products  30.3 us (12%)
  between operations  13.5 us (5%)
  starting transfers between devices  4.24 us (2%)
    reduce_scatter x1, waiting for transfers between devices, shards(): lax.psum_scatter(jnp.einsum('kmc,kcn->mn', masked, integrals, preferred_e...  105 us
    all_to_all x1, blocking collectives, shards(): lax.all_to_all(lax.all_to_all(blocks, 'amp', split_axis=1, concat_axis=1,...  32.7 us
    dot_general x1, matrix products, shards(): jnp.einsum('kmc,kcn->mn', masked, integrals, preferred_element_type=jnp.f...  19.2 us
    all_to_all x1, blocking collectives, shards(): lax.all_to_all(blocks, 'amp', split_axis=1, concat_axis=1, tiled=True)  18.4 us
    convert_element_type x1, local copies, waits for them, and re-layouts, shards(): masked = dense.reshape(k_local, rows, V).astype(jnp.bfloat16)  15.5 us
    dot_general x1, matrix products, shards(): jnp.einsum('krjt,krje->krte', select.astype(jnp.bfloat16), pieces, prefer...  11.1 us
    all_to_all x1, waiting for transfers between devices, shards(): lax.all_to_all(amplitudes, 'amp', split_axis=1, concat_axis=2, tiled=True)  10.9 us
    unnamed x9, local copies, waits for them, and re-layouts  10.6 us
  transfers between devices with their start and end apart: 2, of which 2 were waited for; matrix products, arithmetic and copies ran while one was open for 1% of the time, Pallas kernels for 0%

commit v1 on v0

--- a/solution.py
+++ b/solution.py
@@ -20,7 +20,19 @@
     own_index = lax.axis_index("own")
     n_amp = lax.axis_size("amp")
     n_own = lax.axis_size("own")
-    regrouped = lax.all_to_all(amplitudes, "amp", split_axis=1, concat_axis=2, tiled=True)
+    ways, here = (lax.axis_size("amp"), lax.axis_index("amp"))
+    width = amplitudes.shape[1] // ways
+    dims = list(amplitudes.shape)
+    dims[1] = width
+    height = dims[2]
+    dims[2] = height * ways
+    full = jnp.zeros(dims, amplitudes.dtype)
+    for mask in range(ways):
+        part = lax.dynamic_slice_in_dim(amplitudes, (here ^ mask) * width, width, axis=1)
+        if mask:
+            part = lax.ppermute(part, "amp", [(d, d ^ mask) for d in range(ways)])
+        full = lax.dynamic_update_slice_in_dim(full, part, (here ^ mask) * height, axis=2)
+    regrouped = full
     k_local, rows, packed_width = regrouped.shape
     slot_count = packed_width // TILE
     virt_lab = jnp.repeat(tile_irrep, TILE)

time: 253 us -> 241 us (0.953)
  local copies, waits for them, and re-layouts: 34.7 us -> 24.5 us
    all_to_all x1 -> x0, waiting for transfers between devices: 10.9 us -> none  [shards(): lax.all_to_all(amplitudes, 'amp', split_axis=1, concat_axis=2, tiled=True)]
    unnamed x9 -> x6, local copies, waits for them, and re-layouts: 10.6 us -> 0.01 us
    ppermute x0 -> x3, waiting for transfers between devices: none -> 9.21 us  [shards(): part = lax.ppermute(part, 'amp', [(d, d ^ mask) for d in range(ways)])]
    all_to_all x1 -> x0, starting transfers between devices: 4.24 us -> none  [shards(): lax.all_to_all(amplitudes, 'amp', split_axis=1, concat_axis=2, tiled=True)]
    ppermute x0 -> x3, starting transfers between devices: none -> 3.18 us  [shards(): part = lax.ppermute(part, 'amp', [(d, d ^ mask) for d in range(ways)])]
  transfers between devices with their start and end apart: 2 -> 4, of which waited for: 2 -> 2; matrix products, arithmetic and copies ran while one was open for 1% -> 1% of each run, Pallas kernels for 0% -> 0%
where the time goes in v1:
time: 241 us; the launch traced here: 240 us
  waiting for transfers between devices  115 us (48%)
  blocking collectives  51.2 us (21%)
  matrix products  30.2 us (13%)
  local copies, waits for them, and re-layouts  24.5 us (10%)
  between operations  13.5 us (6%)
  starting transfers between devices  3.18 us (1%)
    reduce_scatter x1, waiting for transfers between devices, shards(): lax.psum_scatter(jnp.einsum('kmc,kcn->mn', masked, integrals, preferred_e...  106 us
    all_to_all x1, blocking collectives, shards(): lax.all_to_all(lax.all_to_all(blocks, 'amp', split_axis=1, concat_axis=1,...  32.7 us
    dot_general x1, matrix products, shards(): jnp.einsum('kmc,kcn->mn', masked, integrals, preferred_element_type=jnp.f...  19.1 us
    all_to_all x1, blocking collectives, shards(): lax.all_to_all(blocks, 'amp', split_axis=1, concat_axis=1, tiled=True)  18.4 us
    convert_element_type x1, local copies, waits for them, and re-layouts, shards(): masked = dense.reshape(k_local, rows, V).astype(jnp.bfloat16)  15.4 us
    dot_general x1, matrix products, shards(): jnp.einsum('krjt,krje->krte', select.astype(jnp.bfloat16), pieces, prefer...  11.1 us
    ppermute x3, waiting for transfers between devices, shards(): part = lax.ppermute(part, 'amp', [(d, d ^ mask) for d in range(ways)])  9.21 us
  transfers between devices with their start and end apart: 4, of which 2 were waited for; matrix products, arithmetic and copies ran while one was open for 1% of the time, Pallas kernels for 0%

profile of v1, /device:TPU:0, one launch (start us, length us, event | category | flops | bytes accessed | tf_op | source)
XLA Modules:
  0.0 240.2 jit_solution(1655423696086155328)
XLA Ops:
  6.5 0.0 reduce-scatter.2.cloned.1.call-start
  6.5 0.1 broadcast_in_dim.8
  6.6 1.8 constant_dynamic-slice_fusion
  8.4 2.4 %collective-permute-start.2 = (bf16[4,576,48]{1,2,0:T(8,128)(2,1)S(1)}, bf16[4,576,48]{1,2,0:T(8,128)(2,1)S(1)}, u32[]{:S(2)}, u32[]{:S(2)}) collective-permute-start(bf16[4,576,48]{1,2,0:T(8,128)(2,1)S(1)} %get-tuple-element.5), channel_id=1, source_target_pairs={{0,24},{8,16},{16,8},{24,0},{1,25},{9,17},{17,9},{25,1},{2,26},{10... | collective-permute-start | bytes 663560 | tf_op jit(solution)/shard_map/ppermute | solution.py:33
  10.8 0.7 collective-permute-start
  11.5 0.0 collective-permute-start.1
  11.6 0.0 copy-done.1
  11.6 0.2 convert_reduce_fusion
  11.7 0.1 broadcast_in_dim.7
  11.8 0.1 tile.8
  11.9 0.1 dynamic_slice.18
  12.0 0.1 broadcast_xor_fusion.1
  12.1 0.1 dynamic_slice.19
  12.1 0.1 broadcast_xor_fusion
  12.2 1.1 broadcast_compare_fusion
  13.3 0.0 collective-permute-done
  13.4 9.2 %collective-permute-done.1 = bf16[4,576,48]{1,2,0:T(8,128)(2,1)S(1)} collective-permute-done((bf16[4,576,48]{1,2,0:T(8,128)(2,1)S(1)}, bf16[4,576,48]{1,2,0:T(8,128)(2,1)S(1)}, u32[]{:S(2)}, u32[]{:S(2)}) %collective-permute-start.1) | collective-permute-done | bytes 221216 | tf_op jit(solution)/shard_map/ppermute | solution.py:33
  22.6 0.0 collective-permute-done.2
  22.7 1.5 copy.20
  24.2 11.1 %convolution_convert_fusion = bf16[4,576,18,64]{3,2,1,0:T(8,128)(2,1)} fusion(bf16[4,576,3,64]{3,2,1,0:T(4,128)(2,1)S(1)} %copy.20, pred[3,18]{1,0:T(4,128)(4,1)S(1)} %iota_compare_fusion.1, pred[4,576,18]{2,1,0:T(8,128)(4,1)} %broadcast_compare_fusion), kind=kOutput, calls=%fused_computation | convolution fusion | flops 18703872 | bytes 6234678 | tf_op jit(solution)/shard_map/krjt,krje->krte/dot_general | solution.py:49
  35.3 15.4 %copy.21 = bf16[4,576,18,64]{1,3,2,0:T(8,128)(2,1)} copy(bf16[4,576,18,64]{3,2,1,0:T(8,128)(2,1)} %convolution_convert_fusion) | data formatting | bytes 10616832 | tf_op jit(solution)/shard_map/convert_element_type | solution.py:52
  50.7 19.1 %convolution_bitcast_fusion = f32[576,2304]{1,0:T(8,128)} fusion(bf16[4,576,1152]{1,2,0:T(8,128)(2,1)} %bitcast.11, bf16[4,1152,2304]{2,1,0:T(8,128)(2,1)} %param.5), kind=kOutput, calls=%fused_computation.1 | convolution fusion | flops 12230590464 | bytes 31850496 | tf_op jit(solution)/shard_map/kmc,kcn->mn/dot_general | solution.py:54
  69.8 0.0 reduce-scatter.2.cloned.1.call-update
  69.8 106.2 %reduce-scatter.2.cloned.1.call-done = f32[72,2304]{1,0:T(8,128)} async-done(((f32[576,2304]{1,0:T(8,128)}), f32[72,2304]{1,0:T(8,128)}) %reduce-scatter.2.cloned.1.call-update) | async-done | bytes 663568 | tf_op jit(solution)/shard_map/reduce_scatter | solution.py:53
  176.1 2.3 reshape.76
  178.4 0.9 copy.23
  179.3 18.4 %all_to_all.10 = f32[72,4,8,72]{0,2,3,1:T(8,128)S(1)} all-to-all(f32[72,4,8,72]{0,2,3,1:T(8,128)S(1)} %copy.23), channel_id=1, replica_groups=mesh['amp'=4,'own'=8] {'amp'}, dimensions={1} | all-to-all | bytes 1327104 | tf_op jit(solution)/shard_map/all_to_all | solution.py:62
  197.8 0.8 copy.24
  198.5 32.7 %all_to_all.11 = f32[72,4,8,72]{0,1,3,2:T(4,128)S(1)} all-to-all(f32[72,4,8,72]{0,1,3,2:T(4,128)S(1)} %copy.24), channel_id=1, replica_groups=mesh['amp'=4,'own'=8] {'own'}, dimensions={2} | all-to-all | bytes 1327104 | tf_op jit(solution)/shard_map/all_to_all | solution.py:61
  231.3 0.7 copy.25
  231.9 0.6 reshape.77
  232.6 0.8 add_convert_fusion
  (10 shorter events, 0.1 us)
Async XLA Ops:
  6.5 5.0 %copy-start.1 = (s32[18]{0:T(128)S(1)}, s32[18]{0:T(128)}, u32[]{:S(2)}) copy-start(s32[18]{0:T(128)} %param.7) | copy-start | bytes 220
  6.5 5.4 %copy-start.2 = (s32[34]{0:T(128)S(1)}, s32[34]{0:T(128)}, u32[]{:S(2)}) copy-start(s32[34]{0:T(128)} %param.6) | copy-start | bytes 412
  6.5 169.5 %reduce-scatter.2.cloned.1.call-start = ((), (), s32[]{:S(2)}) async-start(), calls=%async_computation.3 | async-start | bytes 5971968 | tf_op jit(solution)/shard_map/reduce_scatter | solution.py:53
  8.4 14.3 %collective-permute-start.2 = (bf16[4,576,48]{1,2,0:T(8,128)(2,1)S(1)}, bf16[4,576,48]{1,2,0:T(8,128)(2,1)S(1)}, u32[]{:S(2)}, u32[]{:S(2)}) collective-permute-start(bf16[4,576,48]{1,2,0:T(8,128)(2,1)S(1)} %get-tuple-element.5), channel_id=1, source_target_pairs={{0,24},{8,16},{16,8},{24,0},{1,25},{9,17},{17,9},{25,1},{2,26},{10... | collective-permute-start | bytes 663560 | tf_op jit(solution)/shard_map/ppermute | solution.py:33
  10.8 2.5 %collective-permute-start = (bf16[4,576,48]{1,2,0:T(8,128)(2,1)S(1)}, bf16[4,576,48]{1,2,0:T(8,128)(2,1)S(1)}, u32[]{:S(2)}, u32[]{:S(2)}) collective-permute-start(bf16[4,576,48]{1,2,0:T(8,128)(2,1)S(1)} %get-tuple-element.6), channel_id=1, source_target_pairs={{0,8},{8,0},{16,24},{24,16},{1,9},{9,1},{17,25},{25,17},{2,10},{10... | collective-permute-start | bytes 663560 | tf_op jit(solution)/shard_map/ppermute | solution.py:33
  11.5 11.1 %collective-permute-start.1 = (bf16[4,576,48]{1,2,0:T(8,128)(2,1)S(1)}, bf16[4,576,48]{1,2,0:T(8,128)(2,1)S(1)}, u32[]{:S(2)}, u32[]{:S(2)}) collective-permute-start(bf16[4,576,48]{1,2,0:T(8,128)(2,1)S(1)} %get-tuple-element.8), channel_id=1, source_target_pairs={{0,16},{8,24},{16,0},{24,8},{1,17},{9,25},{17,1},{25,9},{2,18},{10... | collective-permute-start | bytes 663560 | tf_op jit(solution)/shard_map/ppermute | solution.py:33
  231.3 1.3 copy-start
Sparse Core Ops, SparseCore 0:
  70.0 106.0 reduce-scatter.1
